TPU v7x, 512 devices: a whole 4x8x8 slice. The times are simulated.
512 devices in a mesh: head: 8 (over y), ctx: 16 (over z, core), rep: 4 (over x).
Axes of the slice: x: 4, y: 8, z: 8, core: 2. Of those that a mesh axis runs over, the one named last changes fastest.
Arguments:
- inputs: bfloat16 [4, 8192, 8192], P('rep', 'ctx', 'head'), may hold values from -6 to 6
- b_proj: bfloat16 [4, 8192, 2048], P('rep', 'ctx', 'head'), may hold values from -0.375 to 0.375
- c_proj: bfloat16 [4, 8192, 2048], P('rep', 'ctx', 'head'), may hold values from -0.375 to 0.375
- log_decay: bfloat16 [4, 128, 8192], P('rep', 'head', 'ctx'), may hold values from -1 to 0
- starts: int32 [4, 8192], P('rep', 'ctx'), may hold values 0 or 1
- counts: int32 [4, 16], P('rep', 'ctx'), may hold values from 0 to 512, as said below
- skip_gain: float32 [128], P('head'), may hold values from 0.5 to 1.5
- readout: bfloat16 [8192], P('head'), may hold values from -0.0625 to 0.0625
Outputs:
- ssd_out: bfloat16 [4, 8192, 8192], P('rep', 'ctx', 'head')
- token_scores: float32 [4, 8192], P('rep', 'ctx')
Inputs may be any that keep to these rules, and one draw needn't show every extreme that they name: `counts`: at each ctx index, the two rows 2q and 2q + 1 (q = 0, 1, ...) together hold live slots in exactly 2 spans, counting ceil(count / 256) for each; one of the two holds all of them and the other none.
All inputs are finite; a program needn't handle non-finite values. No bound on the sum of `starts` on one device may be relied on, other than what follows from the above.
Results may differ from a plain program's by a relative error of at most 0.0056.
Values may be sent and summed in bfloat16 or wider, within the bound.
A program may use at most 64 MiB of HBM per device.

v0:
```python
import jax
import jax.numpy as jnp
from jax import lax
from jax.sharding import PartitionSpec as P

SPAN = 256
precise = lax.Precision.HIGHEST


def entering_2(value, axis, join, neutral):
    count, mine = (lax.axis_size(axis), lax.axis_index(axis))
    pieces = jax.tree.map(lambda part: lax.all_gather(part, axis), value)
    total = jax.tree.map(
        lambda part, zero: jnp.full_like(part, 0) + jnp.asarray(zero, part.dtype), value, neutral
    )

    def lap(position, total):
        longer = join(total, jax.tree.map(lambda part: part[position], pieces))
        return jax.tree.map(lambda new, old: jnp.where(position < mine, new, old), longer, total)

    return lax.fori_loop(0, count - 1, lap, total)


def span_basics(span_a, span_s):
    length = span_a.shape[-1]
    reset_positions = jnp.arange(length)
    triangle = (reset_positions[:, None] <= reset_positions[None, :]).astype(jnp.float32)
    cum_decay = jnp.dot(span_a.astype(jnp.float32), triangle, precision=precise)
    doc_index = jnp.dot(span_s.astype(jnp.float32), triangle, precision=precise)
    return (reset_positions, cum_decay, doc_index)


def diag_part(span_x, span_b, span_c, span_a, span_s):
    reset_positions, cum_decay, doc_index = span_basics(span_a, span_s)
    head_count = span_a.shape[0]
    length = span_x.shape[0]
    same_doc = (reset_positions[:, None] >= reset_positions[None, :]) & (
        doc_index[:, None] == doc_index[None, :]
    )
    decay_gaps = cum_decay[:, :, None] - cum_decay[:, None, :]
    decay_mat = jnp.where(same_doc, jnp.exp(jnp.minimum(decay_gaps, 0.0)), 0.0)
    scores = jnp.einsum("in,jn->ij", span_c, span_b, preferred_element_type=jnp.float32)
    weights = (decay_mat * scores[None]).astype(jnp.bfloat16)
    per_head = span_x.reshape(length, head_count, -1)
    diag_out = jnp.einsum("hij,jhp->ihp", weights, per_head, preferred_element_type=jnp.float32)
    return diag_out.astype(jnp.bfloat16).reshape(length, -1)


def state_part(span_x, span_b, span_a, span_s):
    reset_positions, cum_decay, doc_index = span_basics(span_a, span_s)
    head_count = span_a.shape[0]
    length = span_x.shape[0]
    last_cum = cum_decay[:, -1]
    end_keep = jnp.where(
        doc_index[None, :] == doc_index[-1], jnp.exp(last_cum[:, None] - cum_decay), 0.0
    )
    weighted_b = (end_keep[:, :, None] * span_b[None].astype(jnp.float32)).astype(jnp.bfloat16)
    per_head = span_x.reshape(length, head_count, -1)
    span_state = jnp.einsum(
        "hjn,jhp->hpn", weighted_b, per_head, preferred_element_type=jnp.float32
    )
    span_total = jnp.where(doc_index[-1] == 0, jnp.exp(last_cum), 0.0)
    entry_keep = jnp.where(doc_index[None, :] == 0, jnp.exp(cum_decay), 0.0)
    return (span_state, span_total, entry_keep)


def combine_carry(earlier, later):
    return (earlier[0] * later[0], later[0][:, None, None] * earlier[1] + later[1])


def local_diag(span_items):
    return lax.map(lambda one_span: diag_part(*one_span), span_items)


def pass_carry(device_pair, start_pair):
    return entering_2(device_pair, "ctx", combine_carry, start_pair)[1]


def within_outputs(x_blocks, b_blocks, c_blocks, a_blocks, s_blocks):
    return local_diag((x_blocks, b_blocks, c_blocks, a_blocks, s_blocks))


def body(inputs, b_proj, c_proj, log_decay, starts, counts, skip_gain, readout):
    tokens = inputs.shape[1]
    length = SPAN
    blocks = tokens // length
    head_count = log_decay.shape[1]
    live_count = counts[0, 0]
    live_mask = jnp.arange(tokens) < live_count
    masked_x = jnp.where(live_mask[:, None], inputs[0], jnp.zeros((), inputs.dtype))
    masked_a = jnp.where(live_mask[None, :], log_decay[0], jnp.zeros((), log_decay.dtype))
    masked_s = jnp.where(live_mask, starts[0], 0)
    x_blocks = masked_x.reshape(blocks, length, -1)
    b_blocks = b_proj[0].reshape(blocks, length, -1)
    c_blocks = c_proj[0].reshape(blocks, length, -1)
    a_blocks = masked_a.reshape(head_count, blocks, length).transpose(1, 0, 2)
    s_blocks = masked_s.reshape(blocks, length)
    state_all, total_all, entry_all = lax.map(
        lambda one_span: state_part(*one_span), (x_blocks, b_blocks, a_blocks, s_blocks)
    )

    def fold_span(carried, span_items):
        total_now, state_now = span_items
        return ((carried[0] * total_now, total_now[:, None, None] * carried[1] + state_now), None)

    start_pair = (jnp.ones((head_count,), jnp.float32), jnp.zeros(state_all.shape[1:], jnp.float32))
    device_pair, unused_out = lax.scan(fold_span, start_pair, (total_all, state_all))
    diag_all = within_outputs(x_blocks, b_blocks, c_blocks, a_blocks, s_blocks)
    diag_all, device_pair = lax.optimization_barrier((diag_all, device_pair))
    carried_in = pass_carry(device_pair, start_pair)

    def enter_span(carried, span_items):
        total_now, state_now = span_items
        return (total_now[:, None, None] * carried + state_now, carried)

    final_state, entering = lax.scan(enter_span, carried_in, (total_all, state_all))
    off_out = jnp.einsum(
        "kin,khpn->kihp",
        c_blocks,
        entering.astype(jnp.bfloat16),
        preferred_element_type=jnp.float32,
    )
    per_head = x_blocks.reshape(blocks, length, head_count, -1)
    mixed_out = diag_all.reshape(blocks, length, head_count, -1).astype(jnp.float32)
    mixed_out = mixed_out + off_out * jnp.transpose(entry_all, (0, 2, 1))[..., None]
    mixed_out = mixed_out + skip_gain[None, None, :, None] * per_head.astype(jnp.float32)
    live_rows = live_mask.reshape(blocks, length).astype(jnp.float32)
    mixed_out = (mixed_out * live_rows[:, :, None, None]).astype(jnp.bfloat16)
    ssd_out = mixed_out.reshape(1, tokens, -1)
    token_part = jnp.dot(ssd_out[0], readout, preferred_element_type=jnp.float32)
    token_scores = lax.psum(token_part, "head")
    return (ssd_out, token_scores.reshape(1, tokens))


def solution(mesh):
    placed = (
        P("rep", "ctx", "head"),
        P("rep", "ctx", "head"),
        P("rep", "ctx", "head"),
        P("rep", "head", "ctx"),
        P("rep", "ctx"),
        P("rep", "ctx"),
        P("head"),
        P("head"),
    )
    return jax.shard_map(
        body,
        mesh=mesh,
        in_specs=placed,
        out_specs=(P("rep", "ctx", "head"), P("rep", "ctx")),
        check_vma=False,
    )
```

profile of v0, /device:TPU:2, one launch (start us, length us, event | category | flops | bytes accessed | tf_op | source)
XLA Modules:
  0.0 198.0 jit_solution(17420713588232635263)
XLA Ops:
  7.3 0.5 broadcast.114
  7.8 1.3 reduce.7
  9.7 2.4 %broadcast_select_fusion.1 = bf16[2,256,1024]{2,1,0:T(8,128)(2,1)} fusion(bf16[2,256,1024]{2,1,0:T(8,128)(2,1)} %bitcast.168, pred[2,256]{1,0:T(4,128)(4,1)S(1)} %get-tuple-element.384), kind=kLoop, calls=%fused_computation.69 | loop fusion | flops 524288 | bytes 2097664 | tf_op jit(solution)/shard_map/jit(_where)/select_n | solution.py:90
  12.2 2.3 %copy.21 = bf16[2,256,1024]{1,2,0:T(8,128)(2,1)} copy(bf16[2,256,1024]{2,1,0:T(8,128)(2,1)} %broadcast_select_fusion.1) | data formatting | bytes 2097152 | tf_op jit(solution)/shard_map/while | solution.py:72
  14.5 9.0 %while.69 = (s32[]{:T(128)}, f32[2,16,64,256]{3,2,1,0:T(8,128)S(1)}, f32[2,16]{1,0:T(2,128)S(1)}, f32[2,16,256]{2,1,0:T(8,128)S(1)}, bf16[2,256,1024]{1,2,0:T(8,...) while((s32[]{:T(128)}, ...), condition=%wide.region_3.4_spmd.clone, body=%wide.region_2.3_spmd.sunk.clone | while | flops 139408144 | bytes 3372799 | solution.py:98
  14.7 0.7 slice.15
  15.4 0.6 broadcast_compare_fusion.4
  16.0 0.2 bitcast_dynamic-update-slice_fusion.6
  16.8 0.2 select_reduce_fusion.3
  17.1 1.1 constant_dynamic-slice_fusion.10
  18.2 0.8 fusion.99
  19.2 0.7 slice.15
  19.9 0.6 broadcast_compare_fusion.4
  21.3 0.2 select_reduce_fusion.3
  21.6 1.1 constant_dynamic-slice_fusion.10
  22.7 0.8 fusion.99
  23.5 0.5 while.71
  23.6 0.2 bitcast_add_fusion.8
  23.8 0.2 bitcast_add_fusion.8
  24.0 1.0 copy-done
  25.0 10.6 %while.68 = (s32[]{:T(128)}, bf16[2,256,1024]{1,2,0:T(8,128)(2,1)}, bf16[2,256,1024]{1,2,0:T(8,128)(2,1)}, s32[2,256]{1,0:T(2,128)S(1)}, bf16[2,16,256]{2,1,0:T(...) while((s32[]{:T(128)}, bf16[2,256,1024]{1,2,0:T(8,128)(2,1)}, ...), condition=%wide.region_1.2_spmd.clone, body=%wide.region_0.1_spmd.sunk.clone | while | flops 176488704 | bytes 12497045 | solution.py:72
  25.0 1.1 fusion.91
  26.1 1.1 constant_dynamic-slice_fusion.9
  27.7 1.6 fusion.95
  29.3 1.0 copy-done.7
  30.3 1.1 fusion.91
  31.4 1.1 constant_dynamic-slice_fusion.9
  32.9 1.6 fusion.95
  34.6 1.0 copy-done.7
  35.6 4.0 %reshape.119 = bf16[2,256,16,64]{3,2,1,0:T(8,128)(2,1)} reshape(bf16[1,512,1024]{2,1,0:T(8,128)(2,1)} %param.18) | data formatting | bytes 2097152 | tf_op jit(solution)/shard_map/squeeze | solution.py:90
  39.6 1.3 dynamic-slice
  41.5 0.2 dynamic-update-slice
  41.8 34.5 %all-reduce = f32[256]{0:T(256)S(1)} all-reduce(f32[256]{0:T(256)S(1)} %dynamic-update-slice), channel_id=2, replica_groups=mesh['head'=8,'ctx'=16,'rep'=4] {'ctx'}, use_global_device_ids=true, to_apply=%add | all-reduce | flops 256 | bytes 2048
  76.3 3.7 %copy.26 = bf16[2,256,16,64]{1,3,2,0:T(8,128)(2,1)} copy(bf16[2,256,16,64]{3,2,1,0:T(8,128)(2,1)} %reshape.119) | data formatting | bytes 2097152 | tf_op jit(solution)/shard_map/squeeze | solution.py:90
  80.0 1.1 broadcast_convert_fusion
  81.1 58.3 %all-gather.4.cloned.1.call-done = f32[256,64,256]{2,1,0:T(8,128)} async-done(((f32[16,64,256]{2,1,0:T(8,128)}), f32[256,64,256]{2,1,0:T(8,128)}) %all-gather.4.cloned.1.call-update) | async-done | bytes 16777232 | tf_op jit(solution)/shard_map/all_gather | solution.py:12
  139.4 22.5 %while.72 = (s32[]{:T(128)}, f32[16,64,256]{2,1,0:T(8,128)S(1)}, s32[]{:T(128)}, f32[16,16]{1,0:T(8,128)S(1)}, f32[16,16,64,256]{3,2,1,0:T(8,128)}) while((s32[]{:T(128)}, f32[16,64,256]{2,1,0:T(8,128)S(1)}, s32[]{:T(128)}, f32[16,16]{1,0:T(8,128)S(1)}, f32[16,16,64,256]{3,2,1,0:T(8,128)}) %tuple.153), condition=%wide.region_7.8_spmd.clone.clone, body=%wide.region_6.7_spmd.clone.sunk.clone | while | flops 1048580 | bytes 3146009 | solution.py:21
  139.4 1.5 fusion.102
  140.9 1.5 fusion.102
  142.4 1.5 fusion.102
  143.9 1.5 fusion.102
  145.4 1.5 fusion.102
  146.9 1.5 fusion.102
  148.4 1.5 fusion.102
  149.9 1.5 fusion.102
  151.4 1.5 fusion.102
  152.9 1.5 fusion.102
  154.4 1.5 fusion.102
  155.9 1.5 fusion.102
  157.4 1.5 fusion.102
  158.9 1.5 fusion.102
  160.4 1.5 fusion.102
  161.9 2.3 %while.70 = (s32[]{:T(128)}, f32[16,64,256]{2,1,0:T(8,128)S(1)}, bf16[2,16,64,256]{3,2,1,0:T(8,128)(2,1)}, f32[2,16]{1,0:T(2,128)S(1)}, f32[2,16,64,256]{3,2,1,0:T(8,128)S(1)}) while((s32[]{:T(128)}, f32[16,64,256]{2,1,0:T(8,128)S(1)}, bf16[2,16,64,256]{3,2,1,0:T(8,128)(2,1)}, f32[2,16]{1,0:T(2,128)S(1)}, ...), condition=%wide.region_9.10_spmd.clone, body=%wide.region_8.9_spmd.sunk.clone | while | flops 524290 | bytes 5243653 | solution.py:116
  161.9 0.9 bitcast_dynamic-update-slice_fusion.7
  162.8 0.2 bitcast_add_fusion.7
  163.1 0.8 bitcast_dynamic-update-slice_fusion.7
  163.9 0.2 bitcast_add_fusion.7
  164.2 2.6 %fusion.41 = bf16[2,256,16,64]{1,3,2,0:T(8,128)(2,1)S(1)} fusion(bf16[2,256,16,64]{1,3,2,0:T(8,128)(2,1)} %bitcast.178, bf16[2,256,256,1]{2,1,3,0:T(8,128)(2,1)S(1)} %bitcast.173, f32[2,256]{1,0:T(2,128)S(1)} %get-tuple-element.385, bf16[2,256,16,64]{1,3,2,0:T(8,128)(2,1)} %copy.26, f32[16]{0:T(128)S(1)} %copy-done.8, f32[2,256,16]{1,2,0:T(8,128)S(1)} %bitcast.179, ...), kind=kOutput, calls=%fused_computation.66 | convolution fusion | flops 273154048 | bytes 4491840 | tf_op jit(solution)/shard_map/kin,khpn->kihp/dot_general | solution.py:117
  166.8 2.0 %copy.33 = bf16[2,256,16,64]{3,2,1,0:T(8,128)(2,1)S(1)} copy(bf16[2,256,16,64]{1,3,2,0:T(8,128)(2,1)S(1)} %fusion.41) | data formatting | bytes 2097152
  168.8 2.1 %copy.27 = bf16[2,256,16,64]{1,0,3,2:T(2,128)(2,1)} copy(bf16[2,256,16,64]{1,3,2,0:T(8,128)(2,1)S(1)} %fusion.41) | data formatting | bytes 2097152 | tf_op jit(solution)/shard_map/convert_element_type | solution.py:128
  170.9 2.3 %reshape.120 = bf16[1,512,1024]{2,1,0:T(8,128)(2,1)} reshape(bf16[2,256,16,64]{3,2,1,0:T(8,128)(2,1)S(1)} %copy.33) | data formatting | bytes 2097152
  173.1 0.2 copy.35
  173.4 0.2 fusion.45
  173.6 17.5 %psum.7 = f32[1,512]{1,0:T(1,128)} all-reduce(f32[1,512]{1,0:T(1,128)S(1)} %fusion.45), channel_id=1, replica_groups=mesh['head'=8,'ctx'=16,'rep'=4] {'head'}, use_global_device_ids=true, to_apply=%region_10.11 | all-reduce | flops 512 | bytes 4096 | tf_op jit(solution)/shard_map/psum | solution.py:131
  (73 shorter events, 2.2 us)
Async XLA Ops:
  7.2 132.2 %all-gather.4.cloned.1.call-start = ((), (), s32[]{:S(2)}) async-start(), calls=%async_computation | async-start | bytes 17825792 | tf_op jit(solution)/shard_map/all_gather | solution.py:12
  9.7 4.7 %copy-start.4 = (bf16[1,16,512]{2,1,0:T(8,128)(2,1)S(1)}, bf16[1,16,512]{2,1,0:T(8,128)(2,1)}, u32[]{:S(2)}) copy-start(bf16[1,16,512]{2,1,0:T(8,128)(2,1)} %param.21) | copy-start | bytes 49156
  9.7 4.8 %copy-start.1 = (bf16[1,512,256]{2,1,0:T(8,128)(2,1)S(1)}, bf16[1,512,256]{2,1,0:T(8,128)(2,1)}, u32[]{:S(2)}) copy-start(bf16[1,512,256]{2,1,0:T(8,128)(2,1)} %param.19) | copy-start | bytes 786436
  24.0 1.0 copy-start
  27.7 1.6 copy-start.6
  29.3 1.0 copy-start.7
  32.9 1.6 copy-start.6
  34.6 1.0 copy-start.7
  39.6 40.4 %copy-start.5 = (bf16[1024]{0:T(1024)(128)(2,1)S(1)}, bf16[1024]{0:T(1024)(128)(2,1)}, u32[]{:S(2)}) copy-start(bf16[1024]{0:T(1024)(128)(2,1)} %param.25) | copy-start | bytes 6148
  161.9 2.3 %copy-start.3 = (bf16[2,256,256]{2,1,0:T(8,128)(2,1)S(1)}, bf16[2,256,256]{2,1,0:T(8,128)(2,1)}, u32[]{:S(2)}) copy-start(bf16[2,256,256]{2,1,0:T(8,128)(2,1)} %get-tuple-element.766) | copy-start | bytes 786436
  161.9 2.3 %copy-start.8 = (f32[16]{0:T(128)S(1)}, f32[16]{0:T(128)}, u32[]{:S(2)}) copy-start(f32[16]{0:T(128)} %param.24) | copy-start | bytes 196
  170.9 2.3 %copy-start.2 = (bf16[2,256,16,64]{1,0,3,2:T(2,128)(2,1)S(1)}, bf16[2,256,16,64]{1,0,3,2:T(2,128)(2,1)}, u32[]{:S(2)}) copy-start(bf16[2,256,16,64]{1,0,3,2:T(2,128)(2,1)} %copy.27) | copy-start | bytes 3145732
Sparse Core Ops, SparseCore 0:
  35.7 103.6 all-gather.3
where the time goes:
time: 199 us; the launch traced here: 198 us
  waiting for transfers between devices  58.3 us (29%)
  blocking collectives  52 us (26%)
  other arithmetic  29.8 us (15%)
  local copies, waits for them, and re-layouts  29.4 us (15%)
  between operations  15.5 us (8%)
  matrix products  11 us (6%)
  loops' own time  1.99 us (1%)
    all_gather x1, waiting for transfers between devices, entering_2(): pieces = jax.tree.map(lambda part: lax.all_gather(part, axis), value)  58.3 us
    unnamed x1, blocking collectives  34.5 us
    select_n x15, other arithmetic, lap(): jnp.where(position < mine, new, old)  21.9 us
    psum x1, blocking collectives, body(): token_scores = lax.psum(token_part, 'head')  17.5 us
    squeeze x2, local copies, waits for them, and re-layouts, body(): inputs[0]  7.72 us
    unnamed x22, local copies, waits for them, and re-layouts  7.55 us
    dynamic_slice x4, local copies, waits for them, and re-layouts, body(): lax.map(lambda one_span: state_part(*one_span), (x_blocks, b_blocks, a_bl...  4.33 us
  transfers between devices with their start and end apart: 1, of which 1 were waited for; matrix products, arithmetic and copies ran while one was open for 5% of the time, Pallas kernels for 0%

commit v1 on v0

--- a/solution.py
+++ b/solution.py
@@ -128,7 +128,7 @@
     mixed_out = (mixed_out * live_rows[:, :, None, None]).astype(jnp.bfloat16)
     ssd_out = mixed_out.reshape(1, tokens, -1)
     token_part = jnp.dot(ssd_out[0], readout, preferred_element_type=jnp.float32)
-    token_scores = lax.psum(token_part, "head")
+    token_scores = jnp.sum(lax.all_gather(token_part, "head"), axis=0)
     return (ssd_out, token_scores.reshape(1, tokens))
 
 

time: 199 us -> 206 us (1.035)
  blocking collectives: 52 us -> 58.3 us
    all_gather x0 -> x1, blocking collectives: none -> 23.9 us  [body(): token_scores = jnp.sum(lax.all_gather(token_part, 'head'), axis=0)]
    psum x1 -> x0, blocking collectives: 17.5 us -> none  [body(): token_scores = lax.psum(token_part, 'head')]
where the time goes in v1:
time: 206 us; the launch traced here: 205 us
  waiting for transfers between devices  58.3 us (28%)
  blocking collectives  58.3 us (28%)
  other arithmetic  30.4 us (15%)
  local copies, waits for them, and re-layouts  29 us (14%)
  between operations  15.5 us (8%)
  matrix products  11 us (5%)
    all_gather x1, waiting for transfers between devices, entering_2(): pieces = jax.tree.map(lambda part: lax.all_gather(part, axis), value)  58.3 us
    unnamed x1, blocking collectives  34.5 us
    all_gather x1, blocking collectives, body(): token_scores = jnp.sum(lax.all_gather(token_part, 'head'), axis=0)  23.9 us
    select_n x15, other arithmetic, lap(): jnp.where(position < mine, new, old)  21.9 us
    squeeze x2, local copies, waits for them, and re-layouts, body(): inputs[0]  7.71 us
    unnamed x22, local copies, waits for them, and re-layouts  7.55 us
    dynamic_slice x4, local copies, waits for them, and re-layouts, body(): lax.map(lambda one_span: state_part(*one_span), (x_blocks, b_blocks, a_bl...  4.33 us
  transfers between devices with their start and end apart: 1, of which 1 were waited for; matrix products, arithmetic and copies ran while one was open for 5% of the time, Pallas kernels for 0%

profile of v1, /device:TPU:2, one launch (start us, length us, event | category | flops | bytes accessed | tf_op | source)
XLA Modules:
  0.0 204.5 jit_solution(15919704281530148364)
XLA Ops:
  7.3 0.5 broadcast.114
  7.8 1.3 reduce.8
  9.7 2.4 %broadcast_select_fusion.1 = bf16[2,256,1024]{2,1,0:T(8,128)(2,1)} fusion(bf16[2,256,1024]{2,1,0:T(8,128)(2,1)} %bitcast.172, pred[2,256]{1,0:T(4,128)(4,1)S(1)} %get-tuple-element.384), kind=kLoop, calls=%fused_computation.70 | loop fusion | flops 524288 | bytes 2097664 | tf_op jit(solution)/shard_map/jit(_where)/select_n | solution.py:90
  12.2 2.3 %copy.21 = bf16[2,256,1024]{1,2,0:T(8,128)(2,1)} copy(bf16[2,256,1024]{2,1,0:T(8,128)(2,1)} %broadcast_select_fusion.1) | data formatting | bytes 2097152 | tf_op jit(solution)/shard_map/while | solution.py:72
  14.5 9.0 %while.69 = (s32[]{:T(128)}, f32[2,16,64,256]{3,2,1,0:T(8,128)S(1)}, f32[2,16]{1,0:T(2,128)S(1)}, f32[2,16,256]{2,1,0:T(8,128)S(1)}, bf16[2,256,1024]{1,2,0:T(8,...) while((s32[]{:T(128)}, ...), condition=%wide.region_3.4_spmd.clone, body=%wide.region_2.3_spmd.sunk.clone | while | flops 139408144 | bytes 3372799 | solution.py:98
  14.7 0.7 slice.15
  15.4 0.6 broadcast_compare_fusion.4
  16.8 0.2 select_reduce_fusion.3
  17.1 1.1 constant_dynamic-slice_fusion.10
  18.2 0.8 fusion.98
  19.2 0.7 slice.15
  19.9 0.6 broadcast_compare_fusion.4
  21.3 0.2 select_reduce_fusion.3
  21.6 1.1 constant_dynamic-slice_fusion.10
  22.7 0.8 fusion.98
  23.5 0.5 while.71
  23.6 0.2 bitcast_add_fusion.8
  23.8 0.2 bitcast_add_fusion.8
  24.0 1.0 copy-done
  25.0 10.2 %while.68 = (s32[]{:T(128)}, bf16[2,256,1024]{1,2,0:T(8,128)(2,1)}, bf16[2,256,1024]{1,2,0:T(8,128)(2,1)}, s32[2,256]{1,0:T(2,128)S(1)}, bf16[2,16,256]{2,1,0:T(...) while((s32[]{:T(128)}, bf16[2,256,1024]{1,2,0:T(8,128)(2,1)}, ...), condition=%wide.region_1.2_spmd.clone, body=%wide.region_0.1_spmd.sunk.clone | while | flops 176488704 | bytes 4108889 | solution.py:72
  25.0 1.1 fusion.90
  26.1 1.1 constant_dynamic-slice_fusion.9
  27.6 1.6 fusion.94
  29.2 0.8 constant_dynamic-update-slice_fusion.3
  30.1 1.1 fusion.90
  31.2 1.1 constant_dynamic-slice_fusion.9
  32.7 1.6 fusion.94
  34.3 0.8 constant_dynamic-update-slice_fusion.3
  35.2 4.0 %reshape.123 = bf16[2,256,16,64]{3,2,1,0:T(8,128)(2,1)} reshape(bf16[1,512,1024]{2,1,0:T(8,128)(2,1)} %param.18) | data formatting | bytes 2097152 | tf_op jit(solution)/shard_map/squeeze | solution.py:90
  39.2 1.3 dynamic-slice
  41.1 0.2 dynamic-update-slice
  41.4 34.5 %all-reduce = f32[256]{0:T(256)S(1)} all-reduce(f32[256]{0:T(256)S(1)} %dynamic-update-slice), channel_id=2, replica_groups=mesh['head'=8,'ctx'=16,'rep'=4] {'ctx'}, use_global_device_ids=true, to_apply=%add | all-reduce | flops 256 | bytes 2048
  75.9 3.7 %copy.26 = bf16[2,256,16,64]{1,3,2,0:T(8,128)(2,1)} copy(bf16[2,256,16,64]{3,2,1,0:T(8,128)(2,1)} %reshape.123) | data formatting | bytes 2097152 | tf_op jit(solution)/shard_map/squeeze | solution.py:90
  79.6 1.1 broadcast_convert_fusion
  80.7 58.3 %all-gather.6.cloned.1.call-done = f32[256,64,256]{2,1,0:T(8,128)} async-done(((f32[16,64,256]{2,1,0:T(8,128)}), f32[256,64,256]{2,1,0:T(8,128)}) %all-gather.6.cloned.1.call-update) | async-done | bytes 16777232 | tf_op jit(solution)/shard_map/all_gather | solution.py:12
  139.0 22.5 %while.72 = (s32[]{:T(128)}, f32[16,64,256]{2,1,0:T(8,128)S(1)}, s32[]{:T(128)}, f32[16,16]{1,0:T(8,128)S(1)}, f32[16,16,64,256]{3,2,1,0:T(8,128)}) while((s32[]{:T(128)}, f32[16,64,256]{2,1,0:T(8,128)S(1)}, s32[]{:T(128)}, f32[16,16]{1,0:T(8,128)S(1)}, f32[16,16,64,256]{3,2,1,0:T(8,128)}) %tuple.153), condition=%wide.region_7.8_spmd.clone.clone, body=%wide.region_6.7_spmd.clone.sunk.clone | while | flops 1048580 | bytes 3146009 | solution.py:21
  139.0 1.5 fusion.101
  140.5 1.5 fusion.101
  142.0 1.5 fusion.101
  143.5 1.5 fusion.101
  145.0 1.5 fusion.101
  146.5 1.5 fusion.101
  148.0 1.5 fusion.101
  149.5 1.5 fusion.101
  151.0 1.5 fusion.101
  152.5 1.5 fusion.101
  154.0 1.5 fusion.101
  155.5 1.5 fusion.101
  157.0 1.5 fusion.101
  158.5 1.5 fusion.101
  160.0 1.5 fusion.101
  161.5 2.3 %while.70 = (s32[]{:T(128)}, f32[16,64,256]{2,1,0:T(8,128)S(1)}, bf16[2,16,64,256]{3,2,1,0:T(8,128)(2,1)}, f32[2,16]{1,0:T(2,128)S(1)}, f32[2,16,64,256]{3,2,1,0:T(8,128)S(1)}) while((s32[]{:T(128)}, f32[16,64,256]{2,1,0:T(8,128)S(1)}, bf16[2,16,64,256]{3,2,1,0:T(8,128)(2,1)}, f32[2,16]{1,0:T(2,128)S(1)}, ...), condition=%wide.region_9.10_spmd.clone, body=%wide.region_8.9_spmd.sunk.clone | while | flops 524290 | bytes 5243653 | solution.py:116
  161.5 0.9 bitcast_dynamic-update-slice_fusion.7
  162.4 0.2 bitcast_add_fusion.7
  162.6 0.9 bitcast_dynamic-update-slice_fusion.7
  163.5 0.2 bitcast_add_fusion.7
  163.8 2.6 %fusion.41 = bf16[2,256,16,64]{1,3,2,0:T(8,128)(2,1)S(1)} fusion(bf16[2,256,16,64]{1,3,2,0:T(8,128)(2,1)} %bitcast.42, bf16[2,256,256,1]{2,1,3,0:T(8,128)(2,1)S(1)} %bitcast.177, f32[2,256]{1,0:T(2,128)S(1)} %get-tuple-element.385, bf16[2,256,16,64]{1,3,2,0:T(8,128)(2,1)} %copy.26, f32[16]{0:T(128)S(1)} %copy-done.6, f32[2,256,16]{1,2,0:T(8,128)S(1)} %bitcast.183, ...), kind=kOutput, calls=%fused_computation.66 | convolution fusion | flops 273154048 | bytes 4491840 | tf_op jit(solution)/shard_map/kin,khpn->kihp/dot_general | solution.py:117
  166.4 2.0 copy.33
  168.4 2.1 %copy.27 = bf16[2,256,16,64]{1,0,3,2:T(2,128)(2,1)} copy(bf16[2,256,16,64]{1,3,2,0:T(8,128)(2,1)S(1)} %fusion.41) | data formatting | bytes 2097152 | tf_op jit(solution)/shard_map/convert_element_type | solution.py:128
  170.5 2.3 %reshape.124 = bf16[1,512,1024]{2,1,0:T(8,128)(2,1)} reshape(bf16[2,256,16,64]{3,2,1,0:T(8,128)(2,1)S(1)} %copy.33) | data formatting | bytes 2097152
  172.7 0.2 copy.35
  173.0 0.2 convolution_bitcast_fusion
  173.2 23.9 %all-gather.3 = f32[8,1,512]{2,1,0:T(1,128)S(1)} all-gather(f32[1,1,512]{2,1,0:T(1,128)S(1)} %convolution_bitcast_fusion), channel_id=4, replica_groups=mesh['head'=8,'ctx'=16,'rep'=4] {'head'}, dimensions={0}, use_global_device_ids=true | all-gather | bytes 18432 | tf_op jit(solution)/shard_map/all_gather | solution.py:131
  197.0 0.6 reduce_sum.9
  (66 shorter events, 2.2 us)
Async XLA Ops:
  7.2 131.8 %all-gather.6.cloned.1.call-start = ((), (), s32[]{:S(2)}) async-start(), calls=%async_computation | async-start | bytes 17825792 | tf_op jit(solution)/shard_map/all_gather | solution.py:12
  9.7 4.7 %copy-start.4 = (bf16[1,16,512]{2,1,0:T(8,128)(2,1)S(1)}, bf16[1,16,512]{2,1,0:T(8,128)(2,1)}, u32[]{:S(2)}) copy-start(bf16[1,16,512]{2,1,0:T(8,128)(2,1)} %param.21) | copy-start | bytes 49156
  9.7 4.8 %copy-start.1 = (bf16[1,512,256]{2,1,0:T(8,128)(2,1)S(1)}, bf16[1,512,256]{2,1,0:T(8,128)(2,1)}, u32[]{:S(2)}) copy-start(bf16[1,512,256]{2,1,0:T(8,128)(2,1)} %param.19) | copy-start | bytes 786436
  24.0 1.0 copy-start
  39.2 40.4 %copy-start.5 = (bf16[1024]{0:T(1024)(128)(2,1)S(1)}, bf16[1024]{0:T(1024)(128)(2,1)}, u32[]{:S(2)}) copy-start(bf16[1024]{0:T(1024)(128)(2,1)} %param.25) | copy-start | bytes 6148
  161.5 2.3 %copy-start.3 = (bf16[2,256,256]{2,1,0:T(8,128)(2,1)S(1)}, bf16[2,256,256]{2,1,0:T(8,128)(2,1)}, u32[]{:S(2)}) copy-start(bf16[2,256,256]{2,1,0:T(8,128)(2,1)} %get-tuple-element.766) | copy-start | bytes 786436
  161.5 2.3 %copy-start.6 = (f32[16]{0:T(128)S(1)}, f32[16]{0:T(128)}, u32[]{:S(2)}) copy-start(f32[16]{0:T(128)} %param.24) | copy-start | bytes 196
  170.5 2.3 %copy-start.2 = (bf16[2,256,16,64]{1,0,3,2:T(2,128)(2,1)S(1)}, bf16[2,256,16,64]{1,0,3,2:T(2,128)(2,1)}, u32[]{:S(2)}) copy-start(bf16[2,256,16,64]{1,0,3,2:T(2,128)(2,1)} %copy.27) | copy-start | bytes 3145732
Sparse Core Ops, SparseCore 0:
  35.3 103.6 all-gather.5
